TPU v7x, 32 devices: a whole 2x2x4 slice. The times are simulated.
32 devices in a mesh: wave: 4 (over y, x), row: 8 (over z, core).
Axes of the slice: x: 2, y: 2, z: 4, core: 2. Of those that a mesh axis runs over, the one named last changes fastest.
Arguments:
- plane_waves: float32 [2, 4, 2048, 2048], P(None, 'wave', 'row'), may hold values from -6 to 6
- transmission: float32 [1, 2, 2048, 2048], P(None, None, 'row')
- wave_index: int32 [4, 2], P('wave'), may hold values from -32 to 31
- wave_weight: float32 [4], P('wave'), may hold values from 0.3 to 3
- wave_phase: float32 [4], P('wave'), may hold values from -3.140625 to 3.140625
- probe_pos: int32 [64, 2], replicated, may hold values from 0 to 2047, as said below
Outputs:
- diffraction: float32 [64, 128, 128], P('row', 'wave')
Inputs may be any that keep to these rules, and one draw needn't show every extreme that they name: `probe_pos`: the probes numbered j * 8 to (j + 1) * 8 - 1 have their grid row (first entry) in j * 256 to (j + 1) * 256 - 1; the second entry is the grid column.
All inputs are finite; a program needn't handle non-finite values.
Results may differ from a plain program's by a relative error of at most 0.0003.
Values sent between devices are 32-bit elements; how exact they have to be, the bound alone decides.
No kernel may reach another device: no remote copies, remote signals or barrier semaphores. Data moves between devices by JAX's collectives and lax.ppermute only.
A program may use at most 128 MiB of HBM per device.

v0:
```python
import math
import jax
import jax.numpy as jnp
from jax import lax
from jax.sharding import PartitionSpec as P

GRID = 2048
RADIX = 64
FACTOR = 16
WINDOW = 128
HALF = 64
FRESNEL = 0.1
EXACT_PRECISION = lax.Precision.HIGHEST


def padded(block, sides, width):
    for axis, dim in sides:
        count = lax.axis_size(axis)
        forward = [(i, i + 1) for i in range(count - 1)]
        forward.append((count - 1, 0))
        backward = [(target, source) for source, target in forward]
        low = lax.ppermute(
            lax.slice_in_dim(block, block.shape[dim] - width, None, axis=dim), axis, forward
        )
        high = lax.ppermute(lax.slice_in_dim(block, 0, width, axis=dim), axis, backward)
        block = jnp.concatenate([low, block, high], axis=dim)
    return block


def tables(length, direction_sign):
    indices = jnp.arange(length, dtype=jnp.int32)
    product = indices[:, None] * indices[None, :] % length
    angles = product.astype(jnp.float32) * (2.0 * math.pi / length)
    return (jnp.cos(angles), direction_sign * jnp.sin(angles))


def twiddle(outer_len, direction_sign):
    outer_idx = jnp.arange(outer_len, dtype=jnp.int32)
    inner_idx = jnp.arange(RADIX, dtype=jnp.int32)
    product = outer_idx[:, None] * inner_idx[None, :] % GRID
    angles = product.astype(jnp.float32) * (2.0 * math.pi / GRID)
    return (jnp.cos(angles), direction_sign * jnp.sin(angles))


def complex_product(formula, left_term, right_term):

    def complex_single(first, second):
        return jnp.einsum(formula, first, second, precision=EXACT_PRECISION)

    real_part = complex_single(left_term[0], right_term[0]) - complex_single(
        left_term[1], right_term[1]
    )
    imag_part = complex_single(left_term[0], right_term[1]) + complex_single(
        left_term[1], right_term[0]
    )
    return (real_part, imag_part)


def pointwise_product(left_term, right_term):
    real_part = left_term[0] * right_term[0] - left_term[1] * right_term[1]
    imag_part = left_term[0] * right_term[1] + left_term[1] * right_term[0]
    return (real_part, imag_part)


def forward_last(halves):
    in_shape = halves[0].shape
    outer_len = GRID // RADIX
    reshaped = tuple((member.reshape(in_shape[:-1] + (outer_len, RADIX)) for member in halves))
    section = complex_product("ka,...ab->...kb", tables(outer_len, -1.0), reshaped)
    section = pointwise_product(section, twiddle(outer_len, -1.0))
    section = complex_product("...kb,bq->...kq", section, tables(RADIX, -1.0))
    return tuple((member.reshape(in_shape) for member in section))


def inverse_last(halves):
    in_shape = halves[0].shape
    outer_len = GRID // RADIX
    reshaped = tuple((member.reshape(in_shape[:-1] + (outer_len, RADIX)) for member in halves))
    section = complex_product("...kq,qb->...kb", reshaped, tables(RADIX, 1.0))
    section = pointwise_product(section, twiddle(outer_len, 1.0))
    section = complex_product("ak,...kb->...ab", tables(outer_len, 1.0), section)
    return tuple((member.reshape(in_shape) / GRID for member in section))


def forward_rows(halves):
    in_shape = halves[0].shape
    outer_len = GRID // RADIX
    reshaped = tuple(
        (member.reshape(in_shape[:-2] + (outer_len, RADIX, in_shape[-1])) for member in halves)
    )
    section = complex_product("ka,...abc->...kbc", tables(outer_len, -1.0), reshaped)
    section = pointwise_product(
        section, tuple((member[:, :, None] for member in twiddle(outer_len, -1.0)))
    )
    section = complex_product("...kbc,bq->...kqc", section, tables(RADIX, -1.0))
    return tuple((member.reshape(in_shape) for member in section))


def inverse_rows(halves):
    in_shape = halves[0].shape
    outer_len = GRID // RADIX
    reshaped = tuple(
        (member.reshape(in_shape[:-2] + (outer_len, RADIX, in_shape[-1])) for member in halves)
    )
    section = complex_product("...kqc,qb->...kbc", reshaped, tables(RADIX, 1.0))
    section = pointwise_product(
        section, tuple((member[:, :, None] for member in twiddle(outer_len, 1.0)))
    )
    section = complex_product("ak,...kbc->...abc", tables(outer_len, 1.0), section)
    return tuple((member.reshape(in_shape) / GRID for member in section))


def permuted_frequency(indices):
    outer_len = GRID // RADIX
    natural = indices // RADIX + outer_len * (indices % RADIX)
    return jnp.where(natural < GRID // 2, natural, natural - GRID)


def propagator_block(first_column, column_count):
    row_freq = permuted_frequency(jnp.arange(GRID, dtype=jnp.int32))
    col_freq = permuted_frequency(first_column + jnp.arange(column_count, dtype=jnp.int32))
    radius = row_freq[:, None] * row_freq[:, None] + col_freq[None, :] * col_freq[None, :]
    phase_angle = radius.astype(jnp.float32) * (math.pi * FRESNEL / GRID)
    inside = 9 * radius <= GRID * GRID
    return (
        jnp.where(inside, jnp.cos(phase_angle), 0.0),
        jnp.where(inside, -jnp.sin(phase_angle), 0.0),
    )


def coefficients(positions, wave_index, wave_weight, wave_phase):
    grid_rows = positions[:, 0:1]
    grid_cols = positions[:, 1:2]
    turns = (
        FACTOR * (grid_rows * wave_index[None, :, 0] + grid_cols * wave_index[None, :, 1]) % GRID
    )
    angles = wave_phase[None, :] - turns.astype(jnp.float32) * (2.0 * math.pi / GRID)
    return (wave_weight[None, :] * jnp.cos(angles), wave_weight[None, :] * jnp.sin(angles))


def wrap_columns(stacked):
    return jnp.concatenate((stacked[..., GRID - HALF :], stacked, stacked[..., :HALF]), axis=-1)


def windows(extended, row_starts, col_starts, weights):
    wave_count = extended.shape[1]

    def windows_single(row_start, col_start, weight_re, weight_im):
        zero_index = jnp.zeros((), jnp.int32)
        window_cut = lax.dynamic_slice(
            extended,
            (zero_index, zero_index, row_start, col_start),
            (2, wave_count, WINDOW, WINDOW),
        )
        real_part = jnp.einsum(
            "w,wij->ij", weight_re, window_cut[0], precision=EXACT_PRECISION
        ) - jnp.einsum("w,wij->ij", weight_im, window_cut[1], precision=EXACT_PRECISION)
        imag_part = jnp.einsum(
            "w,wij->ij", weight_re, window_cut[1], precision=EXACT_PRECISION
        ) + jnp.einsum("w,wij->ij", weight_im, window_cut[0], precision=EXACT_PRECISION)
        return jnp.stack((real_part, imag_part))

    return jax.vmap(windows_single)(row_starts, col_starts, weights[0], weights[1])


def along_cols(halves, dft_table):
    return complex_product("...ij,jk->...ik", halves, dft_table)


def along_rows(halves, dft_table):
    return complex_product("ki,...ij->...kj", dft_table, halves)


def shards(plane_waves, transmission, wave_index, wave_weight, wave_phase, probe_pos):
    rows_here = plane_waves.shape[2]
    row_rank = lax.axis_index("row")
    row_count = lax.axis_size("row")
    propagator_values = propagator_block(row_rank * rows_here, rows_here)
    fields = (plane_waves[0], plane_waves[1])
    fields = pointwise_product(fields, (transmission[0, 0], transmission[0, 1]))
    fields = forward_last(fields)
    column_block = lax.all_to_all(jnp.stack(fields), "row", split_axis=3, concat_axis=2, tiled=True)
    halves = forward_rows((column_block[0], column_block[1]))
    halves = pointwise_product(halves, propagator_values)
    halves = inverse_rows(halves)
    exchanged = lax.all_to_all(jnp.stack(halves), "row", split_axis=2, concat_axis=3, tiled=True)
    fields = inverse_last((exchanged[0], exchanged[1]))
    stacked = jnp.stack(fields)
    probe_count = probe_pos.shape[0] // row_count
    extended = padded(stacked, (("row", 2),), HALF)
    extended = wrap_columns(extended)
    own_probes = lax.dynamic_slice_in_dim(probe_pos, row_rank * probe_count, probe_count, 0)
    row_starts = own_probes[:, 0] - row_rank * rows_here
    weights = coefficients(own_probes, wave_index, wave_weight, wave_phase)
    partial_value = windows(extended, row_starts, own_probes[:, 1], weights)
    dft_table = tables(WINDOW, -1.0)
    halves = (partial_value[:, 0], partial_value[:, 1])
    wave_count = lax.axis_size("wave")
    half_done = along_rows(halves, dft_table)
    summed = lax.psum_scatter(jnp.stack(half_done, axis=1), "wave", scatter_dimension=2, tiled=True)
    summed = jnp.stack(along_cols((summed[:, 0], summed[:, 1]), dft_table), axis=1)
    total_waves = plane_waves.shape[1] * wave_count
    return (summed[:, 0] * summed[:, 0] + summed[:, 1] * summed[:, 1]) / (
        WINDOW * WINDOW * total_waves
    )


def solution(mesh):
    return jax.shard_map(
        shards,
        mesh=mesh,
        in_specs=(
            P(None, "wave", "row", None),
            P(None, None, "row", None),
            P("wave", None),
            P("wave"),
            P("wave"),
            P(),
        ),
        out_specs=P("row", "wave", None),
        check_vma=False,
    )
```

profile of v0, /device:TPU:0, one launch (start us, length us, event | category | flops | bytes accessed | tf_op | source)
XLA Modules:
  0.0 549.7 jit_solution(2807459312730513669)
XLA Ops:
  6.5 3.9 fusion.454
  13.4 4.8 fusion.453
  25.8 4.0 multiply_subtract_fusion.1
  29.8 4.6 fusion.67
  34.4 4.6 fusion.65
  39.3 5.0 fusion.73
  44.3 4.6 fusion.30
  48.9 3.3 fusion.59
  52.3 3.3 fusion.57
  55.6 3.6 fusion.79
  59.2 8.6 %copy.196 = f32[1,1,256,2048]{2,0,1,3:T(1,128)S(1)} copy(f32[1,1,256,2048]{2,3,1,0:T(8,128)S(1)} %bitcast.331) | data formatting | bytes 4194304 | tf_op jit(solution)/shard_map/stack;reshape | solution.py:182
  67.8 3.4 fusion.82
  71.1 8.6 %copy.197 = f32[1,1,256,2048]{2,0,1,3:T(1,128)S(1)} copy(f32[1,1,256,2048]{2,3,1,0:T(8,128)S(1)} %bitcast.330) | data formatting | bytes 4194304 | tf_op jit(solution)/shard_map/stack;reshape | solution.py:182
  79.7 5.0 pad_maximum_fusion.6
  84.7 6.3 %all-to-all-start = ((f32[2,1,256,2048]{2,0,1,3:T(2,128)}), f32[2,1,256,2048]{2,0,1,3:T(2,128)}, u32[]{:S(2)}, u32[]{:S(2)}) async-start(f32[2,1,256,2048]{2,0,1,3:T(2,128)} %pad_maximum_fusion.6), calls=%async_computation | async-start | bytes 8388608 | tf_op jit(solution)/shard_map/all_to_all | solution.py:182
  91.1 94.0 %all-to-all-done = f32[2,1,256,2048]{2,0,1,3:T(2,128)} async-done(((f32[2,1,256,2048]{2,0,1,3:T(2,128)}), f32[2,1,256,2048]{2,0,1,3:T(2,128)}, u32[]{:S(2)}, u32[]{:S(2)}) %all-to-all-start) | async-done | bytes 4194336 | tf_op jit(solution)/shard_map/all_to_all | solution.py:182
  191.9 4.6 fusion.51
  196.5 4.6 fusion.49
  203.5 5.0 fusion.85
  208.5 4.2 fusion.26
  212.7 3.1 fusion.43
  215.8 3.3 fusion.41
  219.1 3.2 fusion.91
  222.3 3.1 fusion.94
  225.4 10.1 %fusion.139 = f32[64,32,256]{2,0,1:T(8,128)S(1)} fusion(f32[64,32,256]{2,0,1:T(8,128)S(1)} %fusion.94, f32[64,32,256]{2,0,1:T(8,128)S(1)} %fusion.91, s32[256]{0:T(256)S(1)} %fusion.268, s32[32,64]{1,0:T(8,128)S(1)} %fusion.186), kind=kOutput, calls=%fused_computation.177 | convolution fusion | flops 408477696 | bytes 6300672 | tf_op jit(solution)/shard_map/...kqc,qb->...kbc/dot_general | solution.py:48
  235.5 10.3 %fusion.150 = f32[64,32,256]{2,0,1:T(8,128)S(1)} fusion(f32[64,32,256]{2,0,1:T(8,128)S(1)} %fusion.94, f32[64,32,256]{2,0,1:T(8,128)S(1)} %fusion.91, s32[256]{0:T(256)S(1)} %fusion.268, s32[32,64]{1,0:T(8,128)S(1)} %fusion.186), kind=kOutput, calls=%fused_computation.188 | convolution fusion | flops 408477696 | bytes 6300672 | tf_op jit(solution)/shard_map/...kqc,qb->...kbc/dot_general | solution.py:48
  245.9 10.1 %fusion.152 = f32[64,32,256]{2,0,1:T(8,128)S(1)} fusion(f32[64,32,256]{2,0,1:T(8,128)S(1)} %fusion.94, f32[64,32,256]{2,0,1:T(8,128)S(1)} %fusion.91, s32[256]{0:T(256)S(1)} %fusion.268, s32[32,64]{1,0:T(8,128)S(1)} %fusion.186), kind=kOutput, calls=%fused_computation.190 | convolution fusion | flops 408477696 | bytes 6300672 | tf_op jit(solution)/shard_map/...kqc,qb->...kbc/dot_general | solution.py:48
  256.0 10.2 %fusion.141 = f32[64,32,256]{2,0,1:T(8,128)S(1)} fusion(f32[64,32,256]{2,0,1:T(8,128)S(1)} %fusion.94, f32[64,32,256]{2,0,1:T(8,128)S(1)} %fusion.91, s32[256]{0:T(256)S(1)} %fusion.268, s32[32,64]{1,0:T(8,128)S(1)} %fusion.186), kind=kOutput, calls=%fused_computation.179 | convolution fusion | flops 408477696 | bytes 6300672 | tf_op jit(solution)/shard_map/...kqc,qb->...kbc/dot_general | solution.py:48
  266.1 4.7 fusion.24
  282.2 11.7 %copy.218 = f32[2,1,2048,256]{3,1,0,2:T(1,128)} copy(f32[2,1,2048,256]{3,2,1,0:T(8,128)S(1)} %pad_maximum_fusion.7) | data formatting | bytes 8388608 | tf_op jit(solution)/shard_map/stack | solution.py:186
  293.9 4.6 all-to-all-start.1
  298.5 93.9 %all-to-all-done.1 = f32[2,1,2048,256]{3,1,0,2:T(1,128)} async-done(((f32[2,1,2048,256]{3,1,0,2:T(1,128)}), f32[2,1,2048,256]{3,1,0,2:T(1,128)}, u32[]{:S(2)}, u32[]{:S(2)}) %all-to-all-start.1) | async-done | bytes 4194336 | tf_op jit(solution)/shard_map/all_to_all | solution.py:186
  399.3 3.3 fusion.148
  402.7 3.5 fusion.136
  408.3 3.9 convolution_subtract_fusion
  412.2 3.1 multiply_subtract_fusion
  415.3 3.2 fusion.33
  418.6 3.2 fusion.35
  421.8 3.6 multiply_bitcast_fusion
  426.6 3.3 multiply_bitcast_fusion.1
  436.1 3.1 copy.229
  439.3 3.5 collective-permute-start.1
  446.2 14.3 %collective-permute-done = f32[2,1,64,2048]{3,2,1,0:T(8,128)} collective-permute-done((f32[2,1,64,2048]{3,2,1,0:T(8,128)S(1)}, f32[2,1,64,2048]{3,2,1,0:T(8,128)}, u32[]{:S(2)}, u32[]{:S(2)}) %collective-permute-start) | collective-permute-done | bytes 1048608 | tf_op jit(solution)/shard_map/ppermute | solution.py:22
  460.5 3.1 copy.230
  463.6 3.3 copy.231
  466.9 14.8 %fusion = f32[2,1,384,2176]{2,3,1,0:T(8,128)} fusion(f32[2,1,64,2048]{2,3,1,0:T(8,128)} %copy.231, f32[2,1,64,2048]{2,3,1,0:T(8,128)} %copy.230, f32[1,1,256,2048]{2,3,1,0:T(8,128)S(1)} %bitcast.318, f32[1,1,256,2048]{2,3,1,0:T(8,128)} %bitcast.320), kind=kLoop, calls=%fused_computation.4 | loop fusion | flops 18382848 | bytes 12976128 | tf_op jit(solution)/shard_map/concatenate | solution.py:142
  481.7 25.6 %while.1 = (s32[]{:T(128)}, f32[2,1,384,2176]{2,3,1,0:T(8,128)}, s32[8,4]{0,1:T(4,128)S(1)}, f32[8,2,1,128,128]{3,4,0,2,1:T(8,128)S(1)}, s32[]{:T(128)}) while((s32[]{:T(128)}, f32[2,1,384,2176]{2,3,1,0:T(8,128)}, s32[8,4]{0,1:T(4,128)S(1)}, f32[8,2,1,128,128]{3,4,0,2,1:T(8,128)S(1)}, s32[]{:T(128)}) %tuple.44), condition=%wide.while_cond, body=%wide.while_body.sunk | while | flops 2 | bytes 1048701 | solution.py:150
  512.4 26.3 %reduce-scatter.2.cloned.1.call-done = f32[8,2,32,128]{3,0,1,2:T(8,128)} async-done(((f32[8,2,128,128]{3,0,1,2:T(8,128)}), f32[8,2,32,128]{3,0,1,2:T(8,128)}) %reduce-scatter.2.cloned.1.call-update) | async-done | bytes 262160 | tf_op jit(solution)/shard_map/reduce_scatter | solution.py:200
  (118 shorter events, 83.8 us)
Async XLA Ops:
  6.5 436.3 %copy-start = (s32[64,2]{0,1:T(2,128)S(1)}, s32[64,2]{0,1:T(2,128)}, u32[]{:S(2)}) copy-start(s32[64,2]{0,1:T(2,128)} %param.11) | copy-start | bytes 1540
  39.3 5.0 copy-start.2
  84.7 100.4 %all-to-all-start = ((f32[2,1,256,2048]{2,0,1,3:T(2,128)}), f32[2,1,256,2048]{2,0,1,3:T(2,128)}, u32[]{:S(2)}, u32[]{:S(2)}) async-start(f32[2,1,256,2048]{2,0,1,3:T(2,128)} %pad_maximum_fusion.6), calls=%async_computation | async-start | bytes 8388608 | tf_op jit(solution)/shard_map/all_to_all | solution.py:182
  203.5 5.0 copy-start.4
  293.9 98.5 %all-to-all-start.1 = ((f32[2,1,2048,256]{3,1,0,2:T(1,128)}), f32[2,1,2048,256]{3,1,0,2:T(1,128)}, u32[]{:S(2)}, u32[]{:S(2)}) async-start(f32[2,1,2048,256]{3,1,0,2:T(1,128)} %copy.218), calls=%async_computation.1 | async-start | bytes 8388608 | tf_op jit(solution)/shard_map/all_to_all | solution.py:186
  298.5 240.3 %reduce-scatter.2.cloned.1.call-start = ((), (), s32[]{:S(2)}) async-start(), calls=%async_computation.3 | async-start | bytes 1310720 | tf_op jit(solution)/shard_map/reduce_scatter | solution.py:200
  408.3 3.9 copy-start.3
  431.2 2.7 copy-start.1
  436.0 8.1 %copy-start.6 = (s32[1,2]{1,0:T(1,128)S(1)}, s32[1,2]{1,0:T(1,128)}, u32[]{:S(2)}) copy-start(s32[1,2]{1,0:T(1,128)} %param.8) | copy-start | bytes 28
  436.1 24.4 %collective-permute-start = (f32[2,1,64,2048]{3,2,1,0:T(8,128)S(1)}, f32[2,1,64,2048]{3,2,1,0:T(8,128)}, u32[]{:S(2)}, u32[]{:S(2)}) collective-permute-start(f32[2,1,64,2048]{3,2,1,0:T(8,128)S(1)} %copy.228), channel_id=1, source_target_pairs={{0,1},{1,2},{2,3},{3,4},{4,5},{5,6},{6,7},{7,0},{8,9},{9,10},{10,1... | collective-permute-start | bytes 3145736 | tf_op jit(solution)/shard_map/ppermute | solution.py:22
  439.3 24.4 %collective-permute-start.1 = (f32[2,1,64,2048]{3,2,1,0:T(8,128)}, f32[2,1,64,2048]{3,2,1,0:T(8,128)}, u32[]{:S(2)}, u32[]{:S(2)}) collective-permute-start(f32[2,1,64,2048]{3,2,1,0:T(8,128)} %copy.229), channel_id=1, source_target_pairs={{1,0},{2,1},{3,2},{4,3},{5,4},{6,5},{7,6},{0,7},{9,8},{10,9},{11,1... | collective-permute-start | bytes 3145736 | tf_op jit(solution)/shard_map/ppermute | solution.py:25
  466.9 14.8 %copy-start.5 = (f32[8,2,1,128,128]{3,4,0,2,1:T(8,128)S(1)}, f32[8,2,1,128,128]{3,4,0,2,1:T(8,128)}, u32[]{:S(2)}) copy-start(f32[8,2,1,128,128]{3,4,0,2,1:T(8,128)} %custom-call) | copy-start | bytes 3145732
Sparse Core Ops, SparseCore 0:
  512.6 26.1 reduce-scatter.1
where the time goes:
time: 561 us; the launch traced here: 550 us
  waiting for transfers between devices  229 us (41%)
  matrix products  145 us (26%)
  local copies, waits for them, and re-layouts  112 us (20%)
  other arithmetic  33.4 us (6%)
  between operations  15.7 us (3%)
  starting transfers between devices  14.5 us (3%)
    dot_general x40, matrix products, complex_single(): return jnp.einsum(formula, first, second, precision=EXACT_PRECISION)  145 us
    all_to_all x1, waiting for transfers between devices, shards(): lax.all_to_all(jnp.stack(fields), 'row', split_axis=3, concat_axis=2, til...  94 us
    all_to_all x1, waiting for transfers between devices, shards(): lax.all_to_all(jnp.stack(halves), 'row', split_axis=2, concat_axis=3, til...  93.9 us
    reduce_scatter x1, waiting for transfers between devices, shards(): lax.psum_scatter(jnp.stack(half_done, axis=1), 'wave', scatter_dimension=...  26.3 us
    gather x48, local copies, waits for them, and re-layouts  25.3 us
    another operation x2, local copies, waits for them, and re-layouts, shards(): jnp.stack(fields)  17.1 us
    concatenate x1, other arithmetic, wrap_columns(): jnp.concatenate((stacked[..., GRID - HALF:], stacked, stacked[..., :HALF]...  14.8 us
    ppermute x1, waiting for transfers between devices, padded(): lax.ppermute(lax.slice_in_dim(block, block.shape[dim] - width, None, axis...  14.3 us
  transfers between devices with their start and end apart: 5, of which 4 were waited for; matrix products, arithmetic and copies ran while one was open for 2% of the time, Pallas kernels for 0%

commit v1 on v0

--- a/solution.py
+++ b/solution.py
@@ -179,7 +179,12 @@
     fields = (plane_waves[0], plane_waves[1])
     fields = pointwise_product(fields, (transmission[0, 0], transmission[0, 1]))
     fields = forward_last(fields)
-    column_block = lax.all_to_all(jnp.stack(fields), "row", split_axis=3, concat_axis=2, tiled=True)
+    column_block = jnp.concatenate(
+        lax.all_to_all(
+            jnp.stack(jnp.split(jnp.stack(fields), lax.axis_size("row"), axis=3)), "row", 0, 0
+        ),
+        axis=2,
+    )
     halves = forward_rows((column_block[0], column_block[1]))
     halves = pointwise_product(halves, propagator_values)
     halves = inverse_rows(halves)

time: 561 us -> 561 us (level)
  local copies, waits for them, and re-layouts: 112 us -> 94 us
  matrix products: 145 us -> 159 us
    dot_general x40, matrix products: 145 us -> 159 us  [complex_single(): return jnp.einsum(formula, first, second, precision=EXACT_PRECISION)]
    another operation x2, local copies, waits for them, and re-layouts: 17.1 us -> 4.85 us  [shards(): jnp.stack(fields)]
    unnamed x1 -> x8, other arithmetic: 0.01 us -> 7.09 us
    slice x3 -> x1, local copies, waits for them, and re-layouts: 6.64 us -> 0.39 us  [shards(): halves = forward_rows((column_block[0], column_block[1]))]
where the time goes in v1:
time: 561 us; the launch traced here: 550 us
  waiting for transfers between devices  230 us (41%)
  matrix products  159 us (28%)
  local copies, waits for them, and re-layouts  94 us (17%)
  other arithmetic  36.6 us (7%)
  between operations  15.6 us (3%)
  starting transfers between devices  14.5 us (3%)
    dot_general x40, matrix products, complex_single(): return jnp.einsum(formula, first, second, precision=EXACT_PRECISION)  159 us
    all_to_all x1, waiting for transfers between devices, shards(): lax.all_to_all(jnp.stack(jnp.split(jnp.stack(fields), lax.axis_size('row'...  94 us
    all_to_all x1, waiting for transfers between devices, shards(): lax.all_to_all(jnp.stack(halves), 'row', split_axis=2, concat_axis=3, til...  93.9 us
    reduce_scatter x1, waiting for transfers between devices, shards(): lax.psum_scatter(jnp.stack(half_done, axis=1), 'wave', scatter_dimension=...  28.3 us
    gather x48, local copies, waits for them, and re-layouts  25.7 us
    concatenate x1, other arithmetic, wrap_columns(): jnp.concatenate((stacked[..., GRID - HALF:], stacked, stacked[..., :HALF]...  14.8 us
    ppermute x1, waiting for transfers between devices, padded(): lax.ppermute(lax.slice_in_dim(block, block.shape[dim] - width, None, axis...  14.1 us
    another operation x1, local copies, waits for them, and re-layouts, shards(): jnp.stack(halves)  12.1 us
  transfers between devices with their start and end apart: 5, of which 4 were waited for; matrix products, arithmetic and copies ran while one was open for 2% of the time, Pallas kernels for 0%

profile of v1, /device:TPU:0, one launch (start us, length us, event | category | flops | bytes accessed | tf_op | source)
XLA Modules:
  0.0 550.1 jit_solution(14686526953074682180)
XLA Ops:
  6.5 3.9 fusion.477
  10.5 2.9 copy.219
  13.4 4.8 fusion.476
  22.9 2.9 copy.222
  25.8 4.0 multiply_subtract_fusion.1
  29.9 4.6 fusion.67
  34.5 4.6 fusion.65
  39.4 5.0 fusion.73
  44.4 4.5 fusion.30
  48.9 3.3 fusion.57
  52.2 4.6 fusion.59
  56.9 16.4 %fusion.82 = f32[256,32,64]{0,2,1:T(8,128)} fusion(f32[256,32,64]{0,2,1:T(8,128)S(1)} %fusion.57, f32[256,32,64]{0,1,2:T(8,128)S(1)} %get-tuple-element.43), kind=kOutput, calls=%fused_computation.128 | convolution fusion | flops 403238912 | bytes 6291456 | tf_op jit(solution)/shard_map/...kb,bq->...kq/dot_general | solution.py:48
  75.2 6.8 %fusion.79 = f32[256,32,64]{0,2,1:T(8,128)} fusion(f32[256,32,64]{0,2,1:T(8,128)} %fusion.59, f32[256,32,64]{0,1,2:T(8,128)} %copy-done.2), kind=kOutput, calls=%fused_computation.127 | convolution fusion | flops 403234816 | bytes 6291456 | tf_op jit(solution)/shard_map/...kb,bq->...kq/dot_general | solution.py:48
  82.0 2.9 copy.169
  92.9 6.4 %all-to-all-start = ((f32[8,2,1,256,256]{4,3,2,1,0:T(8,128)}), f32[8,2,1,256,256]{4,3,2,1,0:T(8,128)}, u32[]{:S(2)}, u32[]{:S(2)}) async-start(f32[8,2,1,256,256]{4,3,2,1,0:T(8,128)} %fusion.133), calls=%async_computation | async-start | bytes 8388608 | tf_op jit(solution)/shard_map/all_to_all | solution.py:183
  99.4 94.0 %all-to-all-done = f32[8,2,1,256,256]{4,3,2,1,0:T(8,128)} async-done(((f32[8,2,1,256,256]{4,3,2,1,0:T(8,128)}), f32[8,2,1,256,256]{4,3,2,1,0:T(8,128)}, u32[]{:S(2)}, u32[]{:S(2)}) %all-to-all-start) | async-done | bytes 4194336 | tf_op jit(solution)/shard_map/all_to_all | solution.py:183
  196.3 3.3 fusion.51
  199.6 3.3 fusion.49
  202.9 3.3 fusion.85
  206.2 4.6 fusion.26
  210.8 3.1 fusion.43
  213.9 3.1 fusion.41
  217.0 3.1 fusion.91
  220.1 3.3 fusion.94
  223.5 10.2 %fusion.162 = f32[64,32,256]{2,0,1:T(8,128)S(1)} fusion(f32[64,32,256]{2,0,1:T(8,128)S(1)} %fusion.94, f32[64,32,256]{2,0,1:T(8,128)S(1)} %fusion.91, s32[256]{0:T(256)S(1)} %fusion.291, s32[32,64]{1,0:T(8,128)S(1)} %fusion.209), kind=kOutput, calls=%fused_computation.215 | convolution fusion | flops 408477696 | bytes 6300672 | tf_op jit(solution)/shard_map/...kqc,qb->...kbc/dot_general | solution.py:48
  233.6 9.9 %fusion.173 = f32[64,32,256]{2,0,1:T(8,128)S(1)} fusion(f32[64,32,256]{2,0,1:T(8,128)S(1)} %fusion.94, f32[64,32,256]{2,0,1:T(8,128)S(1)} %fusion.91, s32[256]{0:T(256)S(1)} %fusion.291, s32[32,64]{1,0:T(8,128)S(1)} %fusion.209), kind=kOutput, calls=%fused_computation.226 | convolution fusion | flops 408477696 | bytes 6300672 | tf_op jit(solution)/shard_map/...kqc,qb->...kbc/dot_general | solution.py:48
  243.6 10.3 %fusion.175 = f32[64,32,256]{2,0,1:T(8,128)S(1)} fusion(f32[64,32,256]{2,0,1:T(8,128)S(1)} %fusion.94, f32[64,32,256]{2,0,1:T(8,128)S(1)} %fusion.91, s32[256]{0:T(256)S(1)} %fusion.291, s32[32,64]{1,0:T(8,128)S(1)} %fusion.209), kind=kOutput, calls=%fused_computation.228 | convolution fusion | flops 408477696 | bytes 6300672 | tf_op jit(solution)/shard_map/...kqc,qb->...kbc/dot_general | solution.py:48
  253.9 10.1 %fusion.164 = f32[64,32,256]{2,0,1:T(8,128)S(1)} fusion(f32[64,32,256]{2,0,1:T(8,128)S(1)} %fusion.94, f32[64,32,256]{2,0,1:T(8,128)S(1)} %fusion.91, s32[256]{0:T(256)S(1)} %fusion.291, s32[32,64]{1,0:T(8,128)S(1)} %fusion.209), kind=kOutput, calls=%fused_computation.217 | convolution fusion | flops 408477696 | bytes 6300672 | tf_op jit(solution)/shard_map/...kqc,qb->...kbc/dot_general | solution.py:48
  264.0 5.0 fusion.24
  279.8 12.1 %copy.196 = f32[2,1,2048,256]{3,1,0,2:T(1,128)} copy(f32[2,1,2048,256]{3,2,1,0:T(8,128)S(1)} %pad_maximum_fusion.6) | data formatting | bytes 8388608 | tf_op jit(solution)/shard_map/stack | solution.py:191
  292.0 4.6 all-to-all-start.1
  296.6 93.9 %all-to-all-done.1 = f32[2,1,2048,256]{3,1,0,2:T(1,128)} async-done(((f32[2,1,2048,256]{3,1,0,2:T(1,128)}), f32[2,1,2048,256]{3,1,0,2:T(1,128)}, u32[]{:S(2)}, u32[]{:S(2)}) %all-to-all-start.1) | async-done | bytes 4194336 | tf_op jit(solution)/shard_map/all_to_all | solution.py:191
  397.4 3.4 fusion.171
  400.7 3.5 fusion.159
  406.3 3.9 convolution_subtract_fusion
  410.2 3.1 multiply_subtract_fusion
  413.4 3.2 fusion.33
  416.6 3.2 fusion.35
  419.9 3.6 multiply_bitcast_fusion
  424.7 3.3 multiply_bitcast_fusion.1
  434.2 3.1 copy.207
  437.3 3.5 collective-permute-start.1
  444.4 14.1 %collective-permute-done = f32[2,1,64,2048]{3,2,1,0:T(8,128)} collective-permute-done((f32[2,1,64,2048]{3,2,1,0:T(8,128)S(1)}, f32[2,1,64,2048]{3,2,1,0:T(8,128)}, u32[]{:S(2)}, u32[]{:S(2)}) %collective-permute-start) | collective-permute-done | bytes 1048608 | tf_op jit(solution)/shard_map/ppermute | solution.py:22
  458.5 3.2 copy.208
  461.6 3.3 copy.209
  464.9 14.8 %fusion = f32[2,1,384,2176]{2,3,1,0:T(8,128)} fusion(f32[2,1,64,2048]{2,3,1,0:T(8,128)} %copy.209, f32[2,1,64,2048]{2,3,1,0:T(8,128)} %copy.208, f32[1,1,256,2048]{2,3,1,0:T(8,128)S(1)} %bitcast.364, f32[1,1,256,2048]{2,3,1,0:T(8,128)} %bitcast.366), kind=kLoop, calls=%fused_computation.18 | loop fusion | flops 18382848 | bytes 12976128 | tf_op jit(solution)/shard_map/concatenate | solution.py:142
  479.7 26.1 %while.1 = (s32[]{:T(128)}, f32[2,1,384,2176]{2,3,1,0:T(8,128)}, s32[8,4]{0,1:T(4,128)S(1)}, f32[8,2,1,128,128]{3,4,0,2,1:T(8,128)S(1)}, s32[]{:T(128)}) while((s32[]{:T(128)}, f32[2,1,384,2176]{2,3,1,0:T(8,128)}, s32[8,4]{0,1:T(4,128)S(1)}, f32[8,2,1,128,128]{3,4,0,2,1:T(8,128)S(1)}, s32[]{:T(128)}) %tuple.43), condition=%wide.while_cond, body=%wide.while_body.sunk | while | flops 2 | bytes 1048701 | solution.py:150
  510.9 28.3 %reduce-scatter.2.cloned.1.call-done = f32[8,2,32,128]{3,0,1,2:T(8,128)} async-done(((f32[8,2,128,128]{3,0,1,2:T(8,128)}), f32[8,2,32,128]{3,0,1,2:T(8,128)}) %reduce-scatter.2.cloned.1.call-update) | async-done | bytes 262160 | tf_op jit(solution)/shard_map/reduce_scatter | solution.py:205
  (125 shorter events, 81.8 us)
Async XLA Ops:
  6.5 434.3 %copy-start = (s32[64,2]{0,1:T(2,128)S(1)}, s32[64,2]{0,1:T(2,128)}, u32[]{:S(2)}) copy-start(s32[64,2]{0,1:T(2,128)} %param.11) | copy-start | bytes 1540
  39.4 5.0 copy-start.4
  48.9 8.0 %copy-start.2 = (f32[256,32,64]{0,1,2:T(8,128)}, f32[256,32,64]{0,1,2:T(8,128)S(1)}, u32[]{:S(2)}) copy-start(f32[256,32,64]{0,1,2:T(8,128)S(1)} %get-tuple-element.43) | copy-start | bytes 6291460
  84.9 2.0 copy-start.1
  92.9 100.4 %all-to-all-start = ((f32[8,2,1,256,256]{4,3,2,1,0:T(8,128)}), f32[8,2,1,256,256]{4,3,2,1,0:T(8,128)}, u32[]{:S(2)}, u32[]{:S(2)}) async-start(f32[8,2,1,256,256]{4,3,2,1,0:T(8,128)} %fusion.133), calls=%async_computation | async-start | bytes 8388608 | tf_op jit(solution)/shard_map/all_to_all | solution.py:183
  292.0 98.5 %all-to-all-start.1 = ((f32[2,1,2048,256]{3,1,0,2:T(1,128)}), f32[2,1,2048,256]{3,1,0,2:T(1,128)}, u32[]{:S(2)}, u32[]{:S(2)}) async-start(f32[2,1,2048,256]{3,1,0,2:T(1,128)} %copy.196), calls=%async_computation.1 | async-start | bytes 8388608 | tf_op jit(solution)/shard_map/all_to_all | solution.py:191
  296.5 242.6 %reduce-scatter.2.cloned.1.call-start = ((), (), s32[]{:S(2)}) async-start(), calls=%async_computation.3 | async-start | bytes 1310720 | tf_op jit(solution)/shard_map/reduce_scatter | solution.py:205
  406.3 3.9 copy-start.5
  429.2 2.7 copy-start.3
  434.1 8.1 %copy-start.7 = (s32[1,2]{1,0:T(1,128)S(1)}, s32[1,2]{1,0:T(1,128)}, u32[]{:S(2)}) copy-start(s32[1,2]{1,0:T(1,128)} %param.8) | copy-start | bytes 28
  434.1 24.3 %collective-permute-start = (f32[2,1,64,2048]{3,2,1,0:T(8,128)S(1)}, f32[2,1,64,2048]{3,2,1,0:T(8,128)}, u32[]{:S(2)}, u32[]{:S(2)}) collective-permute-start(f32[2,1,64,2048]{3,2,1,0:T(8,128)S(1)} %copy.206), channel_id=1, source_target_pairs={{0,1},{1,2},{2,3},{3,4},{4,5},{5,6},{6,7},{7,0},{8,9},{9,10},{10,1... | collective-permute-start | bytes 3145736 | tf_op jit(solution)/shard_map/ppermute | solution.py:22
  437.3 24.3 %collective-permute-start.1 = (f32[2,1,64,2048]{3,2,1,0:T(8,128)}, f32[2,1,64,2048]{3,2,1,0:T(8,128)}, u32[]{:S(2)}, u32[]{:S(2)}) collective-permute-start(f32[2,1,64,2048]{3,2,1,0:T(8,128)} %copy.207), channel_id=1, source_target_pairs={{1,0},{2,1},{3,2},{4,3},{5,4},{6,5},{7,6},{0,7},{9,8},{10,9},{11,1... | collective-permute-start | bytes 3145736 | tf_op jit(solution)/shard_map/ppermute | solution.py:25
  464.9 14.8 %copy-start.6 = (f32[8,2,1,128,128]{3,4,0,2,1:T(8,128)S(1)}, f32[8,2,1,128,128]{3,4,0,2,1:T(8,128)}, u32[]{:S(2)}) copy-start(f32[8,2,1,128,128]{3,4,0,2,1:T(8,128)} %custom-call.1) | copy-start | bytes 3145732
Sparse Core Ops, SparseCore 0:
  511.0 28.1 reduce-scatter.1
